TPU v7x, 32 devices: a whole 2x2x4 slice. The times are simulated.
32 devices in a mesh: side: 2 (over core), group: 8 (over z, y), head: 2 (over x).
Axes of the slice: x: 2, y: 2, z: 4, core: 2. Of those that a mesh axis runs over, the one named last changes fastest.
Arguments:
- pool_rows: bfloat16 [2, 768, 4096], P('side', ('group', 'head')), may hold values from -24 to 24
- pool_weight: bfloat16 [2, 4096, 8192], P('side', 'group', 'head'), as said below
- lengths: int32 [8, 3], replicated, may hold values from 1 to 48, 96 in all within a row
- owner: int32 [8, 3], replicated, may hold values from 0 to 7, as said below
Outputs:
- pool_out: bfloat16 [2, 768, 4096], P('side', 'group', 'head')
Inputs may be any that keep to these rules, and one draw needn't show every extreme that they name: owner[p, j] is p with the binary digits of m_j flipped, where m_j = owner[0, j] is the same for every p; the m_j differ between slots, and every binary digit below 8 is set in some m_j. So the 3 requests of a prefill group go to different decode groups, and every decode group receives exactly one request for each slot j. `lengths`: each row sums to 96. `pool_weight`: independent normal entries of deviation 1 / sqrt(4096).
All inputs are finite; a program needn't handle non-finite values.
Results may differ from a plain program's by a relative error of at most 0.0061.
Values may be sent and summed in bfloat16 or wider, within the bound.
A program may use at most 128 MiB of HBM per device.

v0:
```python
import jax
import jax.numpy as jnp
from jax import lax
from jax.sharding import PartitionSpec as P

HEAD_DIM = 256


def shifted(value, axis, by):
    count = lax.axis_size(axis)
    pairs = [(i, i + by) for i in range(count) if 0 <= i + by < count]
    return lax.ppermute(value, axis, pairs)


def on_device(pool_rows, pool_weight, lengths, owner):
    side_index = lax.axis_index("side")
    group_index = lax.axis_index("group")
    requests = lengths.shape[1]
    gathered = lax.all_gather(pool_rows[0], "head", axis=0, tiled=True)
    weight = lax.all_gather(pool_weight[0], "group", axis=0, tiled=True)
    mem_g = gathered.shape[0]
    wide = weight.shape[1] // 2
    heads_dev = wide // HEAD_DIM
    q_req = mem_g // requests
    scale = 1.0 / HEAD_DIM**0.5
    cached = jnp.dot(gathered, weight, preferred_element_type=jnp.float32).astype(jnp.bfloat16)
    queries = cached[:, :wide]
    starts = jnp.cumsum(lengths, axis=1) - lengths
    groups = jnp.arange(lengths.shape[0], dtype=jnp.int32)
    sources, begins, counts = ([], [], [])
    for slot in range(requests):
        hit = owner[:, slot] == group_index
        sources.append(jnp.sum(jnp.where(hit, groups, 0)))
        begins.append(jnp.sum(jnp.where(hit, starts[:, slot], 0)))
        counts.append(jnp.sum(jnp.where(hit, lengths[:, slot], 0)))
    moved = shifted(cached, "side", 1)
    row_slot = jnp.arange(mem_g, dtype=jnp.int32) // q_req
    lower = jnp.zeros((mem_g,), jnp.int32)
    upper = jnp.zeros((mem_g,), jnp.int32)
    for slot in range(requests):
        here = row_slot == slot
        first_row = sources[slot] * mem_g + begins[slot]
        lower = jnp.where(here, first_row, lower)
        upper = jnp.where(here, first_row + counts[slot], upper)
    query_heads = queries.reshape(mem_g, heads_dev, HEAD_DIM)
    piece = lax.all_gather(moved, "group", axis=0, tiled=True)
    running = jnp.full((heads_dev, mem_g), -1e30, jnp.float32)
    count_rows = piece.shape[0]
    key_index = jnp.arange(count_rows, dtype=jnp.int32)
    key_rows = piece[:, :wide].reshape(count_rows, heads_dev, HEAD_DIM)
    value_rows = piece[:, wide:].reshape(count_rows, heads_dev, HEAD_DIM)
    allowed = (key_index[None, :] >= lower[:, None]) & (key_index[None, :] < upper[:, None])
    scores = (
        jnp.einsum("qeh,keh->eqk", query_heads, key_rows, preferred_element_type=jnp.float32)
        * scale
    )
    scores = jnp.where(allowed[None], scores, -1e30)
    newest = jnp.maximum(running, jnp.max(scores, axis=-1))
    expo = jnp.where(allowed[None], jnp.exp(scores - newest[:, :, None]), 0.0)
    total = jnp.sum(expo, axis=-1)
    update = jnp.einsum(
        "eqk,keh->eqh", expo.astype(jnp.bfloat16), value_rows, preferred_element_type=jnp.float32
    )
    accum = update
    running, total, accum = (newest, total, accum)
    mixed = accum / total[:, :, None]
    attended = jnp.transpose(mixed, (1, 0, 2)).reshape(mem_g, wide).astype(jnp.bfloat16)
    partial_out = lax.dot_general(
        attended, weight[:, wide:], (((1,), (1,)), ((), ())), preferred_element_type=jnp.float32
    )
    decoded = lax.psum_scatter(partial_out, "head", scatter_dimension=1, tiled=True).astype(
        jnp.bfloat16
    )
    result = jnp.where(side_index == 0, cached[:, :wide], decoded)
    return result[None]


def solution(mesh):
    placed = (P("side", ("group", "head"), None), P("side", "group", "head"), P(), P())
    return jax.shard_map(
        on_device, mesh=mesh, in_specs=placed, out_specs=P("side", "group", "head"), check_vma=False
    )
```

profile of v0, /device:TPU:0, one launch (start us, length us, event | category | flops | bytes accessed | tf_op | source)
XLA Modules:
  0.0 815.8 jit_solution(10971161938531449910)
XLA Ops:
  6.5 0.0 all-gather.7.cloned.1.call-start
  6.5 0.7 all-gather.7.cloned.1.call-update
  7.3 0.0 all-gather.5.cloned.1.call-start
  7.3 0.2 copy-done.1
  7.5 12.7 %all-gather = bf16[1,96,4096]{2,1,0:T(8,128)(2,1)S(1)} all-gather(bf16[1,48,4096]{2,1,0:T(8,128)(2,1)S(1)} %copy-done.1), channel_id=2, replica_groups=mesh['side'=2,'group'=8,'head'=2] {'head'}, dimensions={1}, use_global_device_ids=true | all-gather | bytes 1179648 | tf_op jit(solution)/shard_map/all_gather | solution.py:19
  20.3 629.0 %all-gather.7.cloned.1.call-done = bf16[1,4096,4096]{2,1,0:T(8,128)(2,1)} async-done(((bf16[1,512,4096]{2,1,0:T(8,128)(2,1)}), bf16[1,4096,4096]{2,1,0:T(8,128)(2,1)}) %all-gather.7.cloned.1.call-update) | async-done | bytes 33554448 | tf_op jit(solution)/shard_map/all_gather | solution.py:20
  649.3 13.4 %convolution_convert_fusion = bf16[96,4096]{1,0:T(8,128)(2,1)S(1)} fusion(bf16[1,96,4096]{2,1,0:T(8,128)(2,1)S(1)} %all-gather, bf16[1,4096,4096]{2,1,0:T(8,128)(2,1)} %all-gather.7.cloned.1.call-done), kind=kOutput, calls=%fused_computation.2 | convolution fusion | flops 3221618688 | bytes 35127296 | tf_op jit(solution)/shard_map/dot_general | solution.py:26
  662.7 1.6 collective-permute-start
  664.3 1.8 collective-permute-done
  666.2 0.9 copy-done
  667.1 0.0 all-gather.5.cloned.1.call-update
  667.1 0.0 reduce-scatter.2.cloned.1.call-start
  667.2 0.0 copy-done.2
  667.2 0.8 fusion.41
  673.7 0.1 fusion.38
  673.9 92.4 %all-gather.5.cloned.1.call-done = bf16[768,4096]{1,0:T(8,128)(2,1)} async-done(((bf16[96,4096]{1,0:T(8,128)(2,1)}), bf16[768,4096]{1,0:T(8,128)(2,1)}) %all-gather.5.cloned.1.call-update) | async-done | bytes 6291472 | tf_op jit(solution)/shard_map/all_gather | solution.py:46
  766.3 3.4 fusion.52
  769.8 1.2 fusion.8
  771.0 0.8 fusion.9
  771.7 1.1 fusion.30
  772.9 9.9 %fusion = f32[96,4096]{1,0:T(8,128)} fusion(bf16[96,2048]{1,0:T(8,128)(2,1)S(1)} %bitcast.91, bf16[4096,4096]{1,0:T(8,128)(2,1)} %bitcast.87), kind=kOutput, calls=%fused_computation | convolution fusion | flops 1610612736 | bytes 18743296 | tf_op jit(solution)/shard_map/dot_general | solution.py:68
  782.8 0.0 reduce-scatter.2.cloned.1.call-update
  782.8 24.5 %reduce-scatter.2.cloned.1.call-done = f32[96,2048]{1,0:T(8,128)} async-done(((f32[96,4096]{1,0:T(8,128)}), f32[96,2048]{1,0:T(8,128)}) %reduce-scatter.2.cloned.1.call-update) | async-done | bytes 786448 | tf_op jit(solution)/shard_map/reduce_scatter | solution.py:71
  807.3 1.9 select_bitcast_fusion
  (11 shorter events, 0.1 us)
Async XLA Ops:
  6.5 1.0 copy-start.1
  6.5 642.8 %all-gather.7.cloned.1.call-start = ((), (), s32[]{:S(2)}) async-start(), calls=%async_computation.3 | async-start | bytes 37748736 | tf_op jit(solution)/shard_map/all_gather | solution.py:20
  7.3 759.1 %all-gather.5.cloned.1.call-start = ((), (), s32[]{:S(2)}) async-start(), calls=%async_computation.1 | async-start | bytes 7077888 | tf_op jit(solution)/shard_map/all_gather | solution.py:46
  20.3 646.9 %copy-start.2 = (s32[8,3]{0,1:T(4,128)S(1)}, s32[8,3]{0,1:T(4,128)}, u32[]{:S(2)}) copy-start(s32[8,3]{0,1:T(4,128)} %param.6) | copy-start | bytes 292
  20.3 647.0 %copy-start.3 = (s32[8,3]{0,1:T(4,128)S(1)}, s32[8,3]{0,1:T(4,128)}, u32[]{:S(2)}) copy-start(s32[8,3]{0,1:T(4,128)} %param.7) | copy-start | bytes 292
  662.7 3.5 collective-permute-start
  666.2 0.9 copy-start
  667.1 140.2 %reduce-scatter.2.cloned.1.call-start = ((), (), s32[]{:S(2)}) async-start(), calls=%async_computation.2 | async-start | bytes 2359296 | tf_op jit(solution)/shard_map/reduce_scatter | solution.py:71
Sparse Core Ops, SparseCore 0:
  8.9 640.3 all-gather.6
  667.3 99.0 all-gather.4
  782.9 24.3 reduce-scatter.1
where the time goes:
time: 816 us
  waiting for transfers between devices  749 us (92%)
  matrix products  25.6 us (3%)
  between operations  18.8 us (2%)
  blocking collectives  12.7 us (2%)
    all_gather x1, waiting for transfers between devices, on_device(): weight = lax.all_gather(pool_weight[0], 'group', axis=0, tiled=True)  629 us
    all_gather x1, waiting for transfers between devices, on_device(): piece = lax.all_gather(moved, 'group', axis=0, tiled=True)  92.4 us
    reduce_scatter x1, waiting for transfers between devices, on_device(): lax.psum_scatter(partial_out, 'head', scatter_dimension=1, tiled=True)  24.5 us
  transfers between devices with their start and end apart: 4, of which 4 were waited for; matrix products, arithmetic and copies ran while one was open for 0% of the time, Pallas kernels for 0%

commit v1 on v0

--- a/solution.py
+++ b/solution.py
@@ -43,7 +43,15 @@
         lower = jnp.where(here, first_row, lower)
         upper = jnp.where(here, first_row + counts[slot], upper)
     query_heads = queries.reshape(mem_g, heads_dev, HEAD_DIM)
-    piece = lax.all_gather(moved, "group", axis=0, tiled=True)
+    piece = jnp.concatenate(
+        lax.all_to_all(
+            jnp.stack([moved for _ in range(lax.axis_size("group"))]),
+            axis_name="group",
+            split_axis=0,
+            concat_axis=0,
+        ),
+        axis=0,
+    )
     running = jnp.full((heads_dev, mem_g), -1e30, jnp.float32)
     count_rows = piece.shape[0]
     key_index = jnp.arange(count_rows, dtype=jnp.int32)

time: 816 us -> 873 us (1.070)
  waiting for transfers between devices: 749 us -> 788 us
  local copies, waits for them, and re-layouts: 4.64 us -> 15.1 us
    all_to_all x0 -> x1, waiting for transfers between devices: none -> 131 us  [on_device(): lax.all_to_all(jnp.stack([moved for _ in range(lax.axis_size('group'))]),...]
    all_gather x1 -> x0, waiting for transfers between devices: 92.4 us -> none  [on_device(): piece = lax.all_gather(moved, 'group', axis=0, tiled=True)]
where the time goes in v1:
time: 873 us
  waiting for transfers between devices  788 us (90%)
  matrix products  26.4 us (3%)
  between operations  19.3 us (2%)
  local copies, waits for them, and re-layouts  15.1 us (2%)
  blocking collectives  12.7 us (1%)
    all_gather x1, waiting for transfers between devices, on_device(): weight = lax.all_gather(pool_weight[0], 'group', axis=0, tiled=True)  629 us
    all_to_all x1, waiting for transfers between devices, on_device(): lax.all_to_all(jnp.stack([moved for _ in range(lax.axis_size('group'))]),...  131 us
    reduce_scatter x1, waiting for transfers between devices, on_device(): lax.psum_scatter(partial_out, 'head', scatter_dimension=1, tiled=True)  25.3 us
  transfers between devices with their start and end apart: 4, of which 4 were waited for; matrix products, arithmetic and copies ran while one was open for 0% of the time, Pallas kernels for 0%

profile of v1, /device:TPU:0, one launch (start us, length us, event | category | flops | bytes accessed | tf_op | source)
XLA Modules:
  0.0 872.8 jit_solution(16257340204348055478)
XLA Ops:
  6.5 0.7 all-gather.4.cloned.1.call-update
  7.3 0.3 copy-done.4
  7.5 12.7 %all-gather = bf16[1,96,4096]{2,1,0:T(8,128)(2,1)S(1)} all-gather(bf16[1,48,4096]{2,1,0:T(8,128)(2,1)S(1)} %copy-done.4), channel_id=2, replica_groups=mesh['side'=2,'group'=8,'head'=2] {'head'}, dimensions={1}, use_global_device_ids=true | all-gather | bytes 1179648 | tf_op jit(solution)/shard_map/all_gather | solution.py:19
  20.3 629.0 %all-gather.4.cloned.1.call-done = bf16[1,4096,4096]{2,1,0:T(8,128)(2,1)} async-done(((bf16[1,512,4096]{2,1,0:T(8,128)(2,1)}), bf16[1,4096,4096]{2,1,0:T(8,128)(2,1)}) %all-gather.4.cloned.1.call-update) | async-done | bytes 33554448 | tf_op jit(solution)/shard_map/all_gather | solution.py:20
  649.3 13.4 %convolution_convert_fusion = bf16[96,4096]{1,0:T(8,128)(2,1)S(1)} fusion(bf16[1,96,4096]{2,1,0:T(8,128)(2,1)S(1)} %all-gather, bf16[1,4096,4096]{2,1,0:T(8,128)(2,1)} %all-gather.4.cloned.1.call-done), kind=kOutput, calls=%fused_computation.2 | convolution fusion | flops 3221618688 | bytes 35127296 | tf_op jit(solution)/shard_map/dot_general | solution.py:26
  662.7 1.6 collective-permute-start
  664.4 1.8 collective-permute-done
  666.2 3.4 stack.2
  669.6 5.0 all-to-all-start
  674.6 0.0 reduce-scatter.2.cloned.1.call-start
  674.7 0.8 fusion.21
  681.3 0.8 fusion.18
  682.1 131.3 %all-to-all-done = bf16[8,96,4096]{2,1,0:T(8,128)(2,1)} async-done(((bf16[8,96,4096]{2,1,0:T(8,128)(2,1)}), bf16[8,96,4096]{2,1,0:T(8,128)(2,1)}, u32[]{:S(2)}, u32[]{:S(2)}) %all-to-all-start) | async-done | bytes 6291488 | tf_op jit(solution)/shard_map/all_to_all | solution.py:47
  813.5 5.4 fusion.32
  818.9 2.8 copy.14
  821.7 3.2 copy.11
  824.9 0.0 copy-start.3
  824.9 1.8 fusion.2
  826.7 0.7 fusion.3
  827.5 1.2 fusion.7
  828.7 10.0 %fusion = f32[96,4096]{1,0:T(8,128)} fusion(bf16[96,2048]{1,0:T(8,128)(2,1)S(1)} %bitcast.78, bf16[4096,4096]{1,0:T(8,128)(2,1)} %bitcast.74), kind=kOutput, calls=%fused_computation | convolution fusion | flops 1610612736 | bytes 18743296 | tf_op jit(solution)/shard_map/dot_general | solution.py:76
  838.7 0.0 reduce-scatter.2.cloned.1.call-update
  838.7 25.3 %reduce-scatter.2.cloned.1.call-done = f32[96,2048]{1,0:T(8,128)} async-done(((f32[96,4096]{1,0:T(8,128)}), f32[96,2048]{1,0:T(8,128)}) %reduce-scatter.2.cloned.1.call-update) | async-done | bytes 786448 | tf_op jit(solution)/shard_map/reduce_scatter | solution.py:79
  864.0 1.9 select_bitcast_fusion
  (19 shorter events, 0.1 us)
Async XLA Ops:
  6.5 1.0 copy-start.4
  6.5 642.8 %all-gather.4.cloned.1.call-start = ((), (), s32[]{:S(2)}) async-start(), calls=%async_computation.3 | async-start | bytes 37748736 | tf_op jit(solution)/shard_map/all_gather | solution.py:20
  662.7 19.4 %copy-start.1 = (bf16[96,4096]{1,0:T(8,128)(2,1)}, bf16[96,4096]{1,0:T(8,128)(2,1)S(1)}, u32[]{:S(2)}) copy-start(bf16[96,4096]{1,0:T(8,128)(2,1)S(1)} %convolution_convert_fusion) | copy-start | bytes 2359300
  662.7 3.5 collective-permute-start
  669.6 5.1 copy-start.5
  669.6 5.2 copy-start.6
  669.6 143.9 %all-to-all-start = ((bf16[8,96,4096]{2,1,0:T(8,128)(2,1)}), bf16[8,96,4096]{2,1,0:T(8,128)(2,1)}, u32[]{:S(2)}, u32[]{:S(2)}) async-start(bf16[8,96,4096]{2,1,0:T(8,128)(2,1)} %stack.2), calls=%async_computation | async-start | bytes 12582912 | tf_op jit(solution)/shard_map/all_to_all | solution.py:47
  674.6 189.4 %reduce-scatter.2.cloned.1.call-start = ((), (), s32[]{:S(2)}) async-start(), calls=%async_computation.2 | async-start | bytes 2359296 | tf_op jit(solution)/shard_map/reduce_scatter | solution.py:79
  824.9 1.9 copy-start.3
  824.9 2.6 copy-start
  828.7 35.3 %copy-start.2 = (bf16[96,4096]{1,0:T(8,128)(2,1)S(1)}, bf16[96,4096]{1,0:T(8,128)(2,1)}, u32[]{:S(2)}) copy-start(bf16[96,4096]{1,0:T(8,128)(2,1)} %copy-done.1) | copy-start | bytes 2359300
Sparse Core Ops, SparseCore 0:
  8.9 640.3 all-gather.3
  838.9 25.0 reduce-scatter.1
